TPU v7x, 32 devices: a whole 2x2x4 slice. The times are simulated.
32 devices in a mesh: wide: 16 (over z, y, x), narrow: 2 (over core).
Axes of the slice: x: 2, y: 2, z: 4, core: 2. Of those that a mesh axis runs over, the one named last changes fastest.
Arguments:
- tokens: bfloat16 [16384, 1024], P(('wide', 'narrow')), may hold values from -6 to 6
- window_span: int32 [32], P('wide'), may hold values from 1 to 2, as said below
- valid_len: int32 [32], P('wide'), may hold values from 384 to 512, as said below
- norm1_gain: float32 [1024], replicated, may hold values from 0.5 to 1.5
- norm1_shift: float32 [1024], replicated, may hold values from -1.8 to 1.8
- w_query: bfloat16 [1024, 1024], P(None, 'narrow'), may hold values from -0.25 to 0.25
- w_key: bfloat16 [1024, 1024], P(None, 'narrow'), may hold values from -0.25 to 0.25
- w_value: bfloat16 [1024, 1024], P(None, 'narrow'), may hold values from -0.1875 to 0.1875
- w_out: bfloat16 [1024, 1024], P('narrow'), may hold values from -1.5 to 1.5
- norm2_gain: float32 [1024], replicated, may hold values from 0.5 to 1.5
- norm2_shift: float32 [1024], replicated, may hold values from -1.8 to 1.8
- w_gate: bfloat16 [1024, 4096], P(None, 'narrow'), may hold values from -0.1875 to 0.1875
- w_up: bfloat16 [1024, 4096], P(None, 'narrow'), may hold values from -0.1875 to 0.1875
- w_down: bfloat16 [4096, 1024], P('narrow'), may hold values from -0.09375 to 0.09375
- cotangent: bfloat16 [16384, 1024], P(('wide', 'narrow')), may hold values from -6 to 6
Outputs:
- out: float32 [16384, 1024], P(('wide', 'narrow'))
- token_grad: float32 [16384, 1024], P(('wide', 'narrow'))
- norm1_gain_grad: float32 [1024], replicated
- norm1_shift_grad: float32 [1024], replicated
- w_query_grad: float32 [1024, 1024], P(None, 'narrow')
- w_key_grad: float32 [1024, 1024], P(None, 'narrow')
- w_value_grad: float32 [1024, 1024], P(None, 'narrow')
- w_out_grad: float32 [1024, 1024], P('narrow')
- norm2_gain_grad: float32 [1024], replicated
- norm2_shift_grad: float32 [1024], replicated
- w_gate_grad: float32 [1024, 4096], P(None, 'narrow')
- w_up_grad: float32 [1024, 4096], P(None, 'narrow')
- w_down_grad: float32 [4096, 1024], P('narrow')
Inputs may be any that keep to these rules, and one draw needn't show every extreme that they name: `window_span`: within each group, blocks 2k and 2k+1 hold the same value: 2 where one window fills both blocks, 1 where each block holds a window of its own. `valid_len`: blocks whose window_span is 2 hold 512.
All inputs are finite; a program needn't handle non-finite values.
Results may differ from a plain program's by a relative error of at most 0.019.
Values may be sent and summed in bfloat16 or wider, within the bound.
A program may use at most 256 MiB of HBM per device.

v0:
```python
import jax
import jax.numpy as jnp
from jax import lax
from jax.sharding import PartitionSpec as P

HD = 64
EPSILON = 1e-05
MASKED = -1e30
ROPE_BASE = 10000.0


def times_transpose(left, right):
    return lax.dot_general(
        left, right, (((1,), (1,)), ((), ())), preferred_element_type=jnp.float32
    )


def transpose_times(left, right):
    return lax.dot_general(
        left, right, (((0,), (0,)), ((), ())), preferred_element_type=jnp.float32
    )


def norm_forward(values, norm_gain, norm_shift):
    average = jnp.mean(values, axis=-1, keepdims=True)
    centred = values - average
    inverse = lax.rsqrt(jnp.mean(centred * centred, axis=-1, keepdims=True) + EPSILON)
    scaled = centred * inverse
    return (scaled * norm_gain + norm_shift, scaled, inverse)


def norm_backward(grad_out, scaled, inverse, norm_gain):
    grad_scaled = grad_out * norm_gain
    first_term = jnp.mean(grad_scaled, axis=-1, keepdims=True)
    second_term = jnp.mean(grad_scaled * scaled, axis=-1, keepdims=True)
    grad_in = inverse * (grad_scaled - first_term - scaled * second_term)
    return (grad_in, jnp.sum(grad_out * scaled, axis=0), jnp.sum(grad_out, axis=0))


def rotary_tables(span_table, block_rows, width):
    row_count = span_table.shape[0] * block_rows
    row_ids = jnp.arange(row_count)
    block_ids = row_ids // block_rows
    span_rows = jnp.repeat(span_table, block_rows)
    position = (row_ids % block_rows + block_rows * (block_ids % 2) * (span_rows == 2)).astype(
        jnp.float32
    )
    columns = jnp.arange(width) % HD
    half_dim = HD // 2
    freq_index = (columns % half_dim).astype(jnp.float32)
    frequency = ROPE_BASE ** (-2.0 * freq_index / HD)
    angles = position[:, None] * frequency[None, :]
    signs = jnp.where(columns < half_dim, -1.0, 1.0).astype(jnp.float32)
    return (jnp.cos(angles), jnp.sin(angles) * signs)


def swap_halves(values):
    row_count = values.shape[0]
    width = values.shape[1]
    parts = values.reshape(row_count, width // HD, 2, HD // 2)
    return jnp.flip(parts, axis=2).reshape(row_count, width)


def rotate(values, cosine, sine_signed):
    return values * cosine + swap_halves(values) * sine_signed


def rotate_back(grads_in, cosine, sine_signed):
    return grads_in * cosine + swap_halves(grads_in * sine_signed)


def pair_mask(block_index, span_table, valid_table, block_rows):
    pair_first = block_index // 2 * 2
    offsets = jnp.arange(2 * block_rows)
    key_block = pair_first + offsets // block_rows
    within = offsets % block_rows
    first_len = lax.dynamic_index_in_dim(valid_table, pair_first, keepdims=False)
    second_len = lax.dynamic_index_in_dim(valid_table, pair_first + 1, keepdims=False)
    own_span = lax.dynamic_index_in_dim(span_table, block_index, keepdims=False)
    length_bound = jnp.where(offsets < block_rows, first_len, second_len)
    return (within < length_bound) & ((own_span == 2) | (key_block == block_index))


def on_device(
    tokens,
    window_span,
    valid_len,
    norm1_gain,
    norm1_shift,
    w_query,
    w_key,
    w_value,
    w_out,
    norm2_gain,
    norm2_shift,
    w_gate,
    w_up,
    w_down,
    cotangent,
):
    local_rows = tokens.shape[0]
    group_rows = local_rows * lax.axis_size("narrow")
    block_count = window_span.shape[0]
    block_rows = group_rows // block_count
    local_width = w_query.shape[1]
    local_heads = local_width // HD
    local_hidden = w_gate.shape[1]
    softmax_scale = HD ** (-0.5)
    token_values = tokens.astype(jnp.float32)
    normed_one, scaled_one, inverse_one = norm_forward(token_values, norm1_gain, norm1_shift)
    normed_one = normed_one.astype(jnp.bfloat16)
    gathered_one = lax.all_gather(normed_one, "narrow", axis=0, tiled=True)
    joined_qkv = jnp.concatenate([w_query, w_key, w_value], axis=1)
    projected = jnp.dot(gathered_one, joined_qkv, preferred_element_type=jnp.float32)
    cosine, sine_signed = rotary_tables(window_span, block_rows, local_width)
    query_rows = (rotate(projected[:, :local_width], cosine, sine_signed) * softmax_scale).astype(
        jnp.bfloat16
    )
    key_rows = rotate(projected[:, local_width : 2 * local_width], cosine, sine_signed).astype(
        jnp.bfloat16
    )
    value_rows = projected[:, 2 * local_width :].astype(jnp.bfloat16)

    def block_slices(block_index):
        query_block = lax.dynamic_slice_in_dim(query_rows, block_index * block_rows, block_rows, 0)
        pair_start = block_index // 2 * 2 * block_rows
        return (
            query_block.reshape(block_rows, local_heads, HD),
            key_rows.reshape(2 * block_rows, local_heads, HD),
            value_rows.reshape(2 * block_rows, local_heads, HD),
            pair_start,
        )

    def masked_scores(block_index, query_block, key_pair):
        scores = jnp.einsum(
            "qhd,khd->hqk", query_block, key_pair, preferred_element_type=jnp.float32
        )
        key_mask = pair_mask(block_index, window_span, valid_len, block_rows)
        return jnp.where(key_mask[None, None, :], scores, MASKED)

    def attend_forward(block_index):
        query_block, key_pair, value_pair, pair_start = block_slices(block_index)
        scores = masked_scores(block_index, query_block, key_pair)
        highest = jnp.max(scores, axis=-1, keepdims=True)
        weights = jnp.exp(scores - highest)
        weight_total = jnp.sum(weights, axis=-1, keepdims=True)
        attention_probs = (weights / weight_total).astype(jnp.bfloat16)
        mixed_block = jnp.einsum(
            "hqk,khd->qhd", attention_probs, value_pair, preferred_element_type=jnp.float32
        )
        return (
            mixed_block.reshape(block_rows, local_width).astype(jnp.bfloat16),
            (highest + jnp.log(weight_total))[:, :, 0],
        )

    mixed_blocks, log_totals = lax.map(attend_forward, jnp.arange(block_count))
    mixed_rows = mixed_blocks.reshape(group_rows, local_width)
    resid_values = token_values + lax.psum_scatter(
        jnp.dot(mixed_rows, w_out, preferred_element_type=jnp.float32),
        "narrow",
        scatter_dimension=0,
        tiled=True,
    )
    normed_two, scaled_two, inverse_two = norm_forward(resid_values, norm2_gain, norm2_shift)
    normed_two = normed_two.astype(jnp.bfloat16)
    gathered_two = lax.all_gather(normed_two, "narrow", axis=0, tiled=True)
    joined_gate_up = jnp.concatenate([w_gate, w_up], axis=1)
    gate_up = jnp.dot(gathered_two, joined_gate_up, preferred_element_type=jnp.float32)
    gate_values = gate_up[:, :local_hidden]
    up_values = gate_up[:, local_hidden:]
    sigmoid_gate = jax.nn.sigmoid(gate_values)
    hidden_rows = (gate_values * sigmoid_gate * up_values).astype(jnp.bfloat16)
    out_values = resid_values + lax.psum_scatter(
        jnp.dot(hidden_rows, w_down, preferred_element_type=jnp.float32).astype(jnp.bfloat16),
        "narrow",
        scatter_dimension=0,
        tiled=True,
    ).astype(jnp.float32)
    shard_rows = lax.all_gather(cotangent, "narrow", axis=0, tiled=True)
    grad_hidden = times_transpose(shard_rows, w_down)
    grad_down_w, grad_hidden = (transpose_times(hidden_rows, shard_rows), grad_hidden)
    silu_grad = sigmoid_gate * (1.0 + gate_values * (1.0 - sigmoid_gate))
    grad_gate_up = jnp.concatenate(
        [grad_hidden * up_values * silu_grad, grad_hidden * gate_values * sigmoid_gate], axis=1
    ).astype(jnp.bfloat16)
    grad_normed_two = lax.psum_scatter(
        times_transpose(grad_gate_up, joined_gate_up), "narrow", scatter_dimension=0, tiled=True
    )
    grad_gate_up_w = transpose_times(gathered_two, grad_gate_up)
    grad_in_two, gain_two_grad, shift_two_grad = norm_backward(
        grad_normed_two, scaled_two, inverse_two, norm2_gain
    )
    grad_resid = cotangent.astype(jnp.float32) + grad_in_two
    shard_rows = lax.all_gather(grad_resid.astype(jnp.bfloat16), "narrow", axis=0, tiled=True)
    grad_mixed_sum = times_transpose(shard_rows, w_out)
    grad_out_w, grad_mixed_sum = (transpose_times(mixed_rows, shard_rows), grad_mixed_sum)
    grad_mixed = grad_mixed_sum.astype(jnp.bfloat16)

    def attend_backward(block_index, running):
        grad_query, grad_key, grad_value = running
        query_block, key_pair, value_pair, pair_start = block_slices(block_index)
        grad_rows = lax.dynamic_slice_in_dim(
            grad_mixed, block_index * block_rows, block_rows, 0
        ).reshape(block_rows, local_heads, HD)
        scores = masked_scores(block_index, query_block, key_pair)
        log_total = lax.dynamic_index_in_dim(log_totals, block_index, keepdims=False)
        attention_probs = jnp.exp(scores - log_total[:, :, None])
        grad_probs = jnp.einsum(
            "qhd,khd->hqk", grad_rows, value_pair, preferred_element_type=jnp.float32
        )
        centre = jnp.sum(attention_probs * grad_probs, axis=-1, keepdims=True)
        grad_scores = (attention_probs * (grad_probs - centre)).astype(jnp.bfloat16)
        block_query = jnp.einsum(
            "hqk,khd->qhd", grad_scores, key_pair, preferred_element_type=jnp.float32
        ).reshape(block_rows, local_width)
        pair_key = jnp.einsum(
            "hqk,qhd->khd", grad_scores, query_block, preferred_element_type=jnp.float32
        ).reshape(2 * block_rows, local_width)
        pair_value = jnp.einsum(
            "hqk,qhd->khd",
            attention_probs.astype(jnp.bfloat16),
            grad_rows,
            preferred_element_type=jnp.float32,
        ).reshape(2 * block_rows, local_width)
        grad_query = lax.dynamic_update_slice_in_dim(
            grad_query, block_query, block_index * block_rows, 0
        )
        grad_key = grad_key + pair_key
        grad_value = grad_value + pair_value
        return (grad_query, grad_key, grad_value)

    zero_rows = jnp.zeros((group_rows, local_width), jnp.float32)
    grad_query, grad_key, grad_value = lax.fori_loop(
        0, block_count, attend_backward, (zero_rows, zero_rows, zero_rows)
    )
    grad_query_raw = rotate_back(grad_query * softmax_scale, cosine, sine_signed)
    grad_key_raw = rotate_back(grad_key, cosine, sine_signed)
    grad_qkv = jnp.concatenate([grad_query_raw, grad_key_raw, grad_value], axis=1).astype(
        jnp.bfloat16
    )
    grad_normed_one = lax.psum_scatter(
        times_transpose(grad_qkv, joined_qkv).astype(jnp.bfloat16),
        "narrow",
        scatter_dimension=0,
        tiled=True,
    ).astype(jnp.float32)
    grad_qkv_w = transpose_times(gathered_one, grad_qkv)
    grad_in_one, gain_one_grad, shift_one_grad = norm_backward(
        grad_normed_one, scaled_one, inverse_one, norm1_gain
    )
    token_grad = grad_resid + grad_in_one
    qkv_summed, out_summed, gate_up_summed, down_summed = (
        lax.psum(grad_qkv_w.astype(jnp.bfloat16), "wide").astype(jnp.float32),
        lax.psum(grad_out_w.astype(jnp.bfloat16), "wide").astype(jnp.float32),
        lax.psum(grad_gate_up_w.astype(jnp.bfloat16), "wide").astype(jnp.float32),
        lax.psum(grad_down_w.astype(jnp.bfloat16), "wide").astype(jnp.float32),
    )
    norm_summed = lax.psum(
        (gain_one_grad, shift_one_grad, gain_two_grad, shift_two_grad), ("wide", "narrow")
    )
    return (
        out_values,
        token_grad,
        norm_summed[0],
        norm_summed[1],
        qkv_summed[:, :local_width],
        qkv_summed[:, local_width : 2 * local_width],
        qkv_summed[:, 2 * local_width :],
        out_summed,
        norm_summed[2],
        norm_summed[3],
        gate_up_summed[:, :local_hidden],
        gate_up_summed[:, local_hidden:],
        down_summed,
    )


def solution(mesh):
    in_specs = (
        P(("wide", "narrow"), None),
        P("wide"),
        P("wide"),
        P(),
        P(),
        P(None, "narrow"),
        P(None, "narrow"),
        P(None, "narrow"),
        P("narrow", None),
        P(),
        P(),
        P(None, "narrow"),
        P(None, "narrow"),
        P("narrow", None),
        P(("wide", "narrow"), None),
    )
    out_specs = (
        P(("wide", "narrow"), None),
        P(("wide", "narrow"), None),
        P(),
        P(),
        P(None, "narrow"),
        P(None, "narrow"),
        P(None, "narrow"),
        P("narrow", None),
        P(),
        P(),
        P(None, "narrow"),
        P(None, "narrow"),
        P("narrow", None),
    )
    return jax.shard_map(
        on_device, mesh=mesh, in_specs=in_specs, out_specs=out_specs, check_vma=False
    )
```

profile of v0, /device:TPU:0, one launch (start us, length us, event | category | flops | bytes accessed | tf_op | source)
XLA Modules:
  0.0 900.9 jit_solution(3977947067159316405)
XLA Ops:
  15.9 10.1 %all-gather.5.cloned.1.call-done = bf16[1024,1024]{1,0:T(8,128)(2,1)} async-done(((bf16[512,1024]{1,0:T(8,128)(2,1)}), bf16[1024,1024]{1,0:T(8,128)(2,1)}) %all-gather.5.cloned.1.call-update) | async-done | bytes 2097168 | tf_op jit(solution)/shard_map/all_gather | solution.py:112
  26.1 5.9 fusion.98
  56.6 11.1 %fusion.54 = (bf16[1024,512]{1,0:T(8,128)(2,1)}, bf16[1024,512]{1,0:T(8,128)(2,1)S(1)}) fusion(f32[1024,512]{1,0:T(8,128)} %copy.42, f32[512]{0:T(512)S(1)} %get-tuple-element.644, f32[512]{0:T(512)S(1)} %get-tuple-element.643, f32[1024]{0:T(1024)S(1)} %fusion.66, f32[1024,1536]{1,0:T(8,128)} %copy-done.15, f32[1024,512]{1,0:T(8,128)} %copy.40), kind=kLoop, calls=%fused_computation.97 | loop fusion | flops 5767168 | bytes 10493952 | tf_op jit(solution)/shard_map/convert_element_type | solution.py:119
  70.5 44.1 %while.36 = (s32[]{:T(128)}, bf16[2,512,512]{2,1,0:T(8,128)(2,1)}, f32[2,8,512]{2,1,0:T(8,128)S(1)}, s32[2]{0:T(128)S(1)}, s32[2]{0:T(128)S(1)}, /*index=5*/s32[...) while((s32[]{:T(128)}, bf16[2,512,512]{2,1,0:T(8,128)(2,1)}, ...), condition=%wide.region_5.6_spmd, body=%wide.region_2.5_spmd.sunk | while | flops 1111768064 | bytes 56758836 | solution.py:156
  86.5 4.9 fusion.162
  108.5 4.9 fusion.162
  114.5 4.5 fusion.99
  119.1 13.3 %reduce-scatter.5.cloned.1.call-done = f32[512,1024]{1,0:T(8,128)} async-done(((f32[1024,1024]{1,0:T(8,128)}), f32[512,1024]{1,0:T(8,128)}) %reduce-scatter.5.cloned.1.call-update) | async-done | bytes 2097168 | tf_op jit(solution)/shard_map/reduce_scatter | solution.py:158
  137.7 4.9 constant_dynamic-update-slice_fusion.6
  149.0 16.4 %fusion.100 = f32[1024,4096]{1,0:T(8,128)} fusion(bf16[1024,1024]{1,0:T(8,128)(2,1)} %all-gather.7.cloned.1.call-done, bf16[1024,4096]{1,0:T(8,128)(2,1)} %constant_dynamic-update-slice_fusion.5), kind=kOutput, calls=%fused_computation.183 | convolution fusion | flops 8589934592 | bytes 27262976 | tf_op jit(solution)/shard_map/dot_general | solution.py:168
  165.5 15.5 %multiply_convert_fusion.2 = (bf16[1024,2048]{1,0:T(8,128)(2,1)S(1)}, bf16[1024,2048]{1,0:T(8,128)(2,1)}, bf16[1024,2048]{1,0:T(8,128)(2,1)}) fusion(f32[1024,4096]{1,0:T(8,128)} %fusion.100, bf16[1024,1024]{1,0:T(8,128)(2,1)} %all-gather.9.cloned.1.call-done, bf16[2048,1024]{1,0:T(8,128)(2,1)} %param.32), kind=kOutput, calls=%fused_computation.59 | convolution fusion | flops 4328521728 | bytes 35651584 | tf_op jit(solution)/shard_map/dot_general | solution.py:13
  182.9 13.9 %fusion.31 = f32[1024,1024]{1,0:T(8,128)} fusion(bf16[1024,4096]{1,0:T(8,128)(2,1)} %constant_dynamic-update-slice_fusion.5, bf16[1024,2048]{1,0:T(8,128)(2,1)} %get-tuple-element.627, bf16[1024,2048]{1,0:T(8,128)(2,1)S(1)} %get-tuple-element.626), kind=kOutput, calls=%fused_computation.63 | convolution fusion | flops 8606711808 | bytes 20971520 | tf_op jit(solution)/shard_map/dot_general | solution.py:13
  196.9 9.3 %convolution_convert_fusion.4 = bf16[1024,1024]{1,0:T(8,128)(2,1)} fusion(bf16[1024,2048]{1,0:T(8,128)(2,1)} %get-tuple-element.628, bf16[2048,1024]{1,0:T(8,128)(2,1)} %param.32), kind=kOutput, calls=%fused_computation.117 | convolution fusion | flops 4296015872 | bytes 10485760 | tf_op jit(solution)/shard_map/dot_general | solution.py:174
  214.0 10.1 %reduce-scatter.7.cloned.1.call-done = bf16[512,1024]{1,0:T(8,128)(2,1)} async-done(((bf16[1024,1024]{1,0:T(8,128)(2,1)}), bf16[512,1024]{1,0:T(8,128)(2,1)}) %reduce-scatter.7.cloned.1.call-update) | async-done | bytes 1048592 | tf_op jit(solution)/shard_map/reduce_scatter | solution.py:173
  224.0 5.8 fusion.88
  229.9 11.9 %all-gather.11.cloned.1.call-done = bf16[1024,1024]{1,0:T(8,128)(2,1)} async-done(((bf16[512,1024]{1,0:T(8,128)(2,1)}), bf16[1024,1024]{1,0:T(8,128)(2,1)}) %all-gather.11.cloned.1.call-update) | async-done | bytes 2097168 | tf_op jit(solution)/shard_map/all_gather | solution.py:194
  247.3 94.5 %while.37 = (s32[]{:T(128)}, f32[1024,512]{1,0:T(8,128)}, f32[1024,512]{0,1:T(8,128)}, f32[1024,512]{0,1:T(8,128)}, s32[2]{0:T(128)S(1)}, /*index=5*/s32[2]{0:T(...) while((s32[]{:T(128)}, f32[1024,512]{1,0:T(8,128)}, ...), condition=%wide.region_15.16_spmd.clone, body=%wide.region_13.15_spmd.clone.sunk | while | flops 2736798720 | bytes 236049072 | solution.py:233
  259.6 9.7 %multiply_reduce_fusion.6 = (f32[8,512]{1,0:T(8,128)S(1)}, f32[8,512,1024]{2,1,0:T(8,128)}) fusion(f32[8,512,1024]{2,1,0:T(8,128)S(1)} %fusion.173, f32[8,512]{1,0:T(8,128)S(1)} %dynamic-slice_bitcast_fusion.2, pred[1024]{0:T(1024)(128)(4,1)S(1)} %fusion.175, bf16[512,8,64]{0,2,1:T(8,128)(2,1)S(1)} %bitcast.141, bf16[1024,8,64]{0,2,1:T(8,128)(2,1)} %bitcast.133), kind=kOutput, calls=%fused_computation.27.clone.1 | convolution fusion | flops 553644032 | bytes 35161088 | tf_op jit(solution)/shard_map/while/body/eval_jaxpr/qhd,khd->hqk/dot_general | solution.py:208
  269.3 10.4 %multiply_convert_fusion.5 = bf16[8,512,1024]{2,1,0:T(8,128)(2,1)} fusion(f32[8,512,1024]{2,1,0:T(8,128)} %get-tuple-element.783, f32[8,512,1024]{2,1,0:T(8,128)S(1)} %fusion.173, f32[8,512]{1,0:T(8,128)S(1)} %get-tuple-element.784, f32[8,512]{1,0:T(8,128)S(1)} %dynamic-slice_bitcast_fusion.2, pred[1024]{0:T(1024)(128)(4,1)S(1)} %fusion.175), kind=kLoop, calls=%fused_computation.26.clone.1 | loop fusion | flops 20971520 | bytes 41976832 | tf_op jit(solution)/shard_map/while/body/eval_jaxpr/convert_element_type | solution.py:212
  279.7 7.2 fusion.176
  306.8 9.7 %multiply_reduce_fusion.6 = (f32[8,512]{1,0:T(8,128)S(1)}, f32[8,512,1024]{2,1,0:T(8,128)}) fusion(f32[8,512,1024]{2,1,0:T(8,128)S(1)} %fusion.173, f32[8,512]{1,0:T(8,128)S(1)} %dynamic-slice_bitcast_fusion.2, pred[1024]{0:T(1024)(128)(4,1)S(1)} %fusion.175, bf16[512,8,64]{0,2,1:T(8,128)(2,1)S(1)} %bitcast.141, bf16[1024,8,64]{0,2,1:T(8,128)(2,1)} %bitcast.133), kind=kOutput, calls=%fused_computation.27.clone.1 | convolution fusion | flops 553644032 | bytes 35161088 | tf_op jit(solution)/shard_map/while/body/eval_jaxpr/qhd,khd->hqk/dot_general | solution.py:208
  316.5 10.4 %multiply_convert_fusion.5 = bf16[8,512,1024]{2,1,0:T(8,128)(2,1)} fusion(f32[8,512,1024]{2,1,0:T(8,128)} %get-tuple-element.783, f32[8,512,1024]{2,1,0:T(8,128)S(1)} %fusion.173, f32[8,512]{1,0:T(8,128)S(1)} %get-tuple-element.784, f32[8,512]{1,0:T(8,128)S(1)} %dynamic-slice_bitcast_fusion.2, pred[1024]{0:T(1024)(128)(4,1)S(1)} %fusion.175), kind=kLoop, calls=%fused_computation.26.clone.1 | loop fusion | flops 20971520 | bytes 41976832 | tf_op jit(solution)/shard_map/while/body/eval_jaxpr/convert_element_type | solution.py:212
  326.9 7.2 fusion.176
  346.0 9.4 %fusion.61 = (f32[1024,512]{1,0:T(8,128)}, f32[1024,512]{1,0:T(8,128)S(1)}) fusion(f32[1024,512]{1,0:T(8,128)} %get-tuple-element.477, f32[512]{0:T(512)S(1)} %copy-done.45, f32[512]{0:T(512)S(1)} %copy-done.43, f32[1024]{0:T(1024)S(1)} %copy-done.34, f32[1024,512]{1,0:T(8,128)} %copy.54), kind=kLoop, calls=%fused_computation.104 | loop fusion | flops 2621440 | bytes 8396800 | tf_op jit(solution)/shard_map/mul | solution.py:69
  372.3 9.1 %fusion.56 = (bf16[1024,512]{1,0:T(8,128)(2,1)S(1)}, bf16[1024,512]{1,0:T(8,128)(2,1)S(1)}) fusion(f32[1024,512]{1,0:T(8,128)} %copy.53, f32[1024,512]{1,0:T(8,128)} %get-tuple-element.477, f32[512]{0:T(512)S(1)} %copy-done.43, f32[1024]{0:T(1024)S(1)} %copy-done.34, f32[1024,512]{1,0:T(8,128)} %copy.57, f32[1024,512]{1,0:T(8,128)S(1)} %copy-done.14), kind=kLoop, calls=%fused_computation.99 | loop fusion | flops 4194304 | bytes 10491904 | tf_op jit(solution)/shard_map/convert
  382.8 4.6 convolution_convert_fusion.3
  389.0 8.7 convolution_convert_fusion.2
  397.7 11.5 %convolution_convert_fusion = bf16[1024,4096]{1,0:T(8,128)(2,1)} fusion(bf16[1024,1024]{1,0:T(8,128)(2,1)S(1)} %copy-done.51, bf16[1024,2048]{1,0:T(8,128)(2,1)S(1)} %copy-done.56, bf16[1024,2048]{1,0:T(8,128)(2,1)S(1)} %copy-done.55), kind=kOutput, calls=%fused_computation.62 | convolution fusion | flops 8610906112 | bytes 18874368 | tf_op jit(solution)/shard_map/dot_general | solution.py:19
  411.6 5.5 convolution_convert_fusion.1
  420.6 44.3 %all-reduce = (f32[1024]{0:T(1024)}, f32[1024]{0:T(1024)}, f32[1024]{0:T(1024)}, f32[1024]{0:T(1024)}) all-reduce(f32[1024]{0:T(1024)S(1)} %get-tuple-element.559, f32[1024]{0:T(1024)S(1)} %get-tuple-element.563, f32[1024]{0:T(1024)S(1)} %copy-done.46, f32[1024]{0:T(1024)S(1)} %copy-done.47), channel_id=1, replica_groups=mesh['wide'=16,'narrow'=2] {'wide','narrow'}, use_global_device_ids=true, to_apply=%region_20.21 | all-reduce | flops 4096 | bytes 32768 | tf_op jit(solution)/shard_map/psum | solution.py:258
  468.7 401.7 %all-reduce.4.cloned.1.call-done = (bf16[1024,1536]{1,0:T(8,128)(2,1)}, bf16[512,1024]{1,0:T(8,128)(2,1)}, bf16[1024,4096]{1,0:T(8,128)(2,1)}, bf16[2048,1024]{1,0:T(8,128)(2,1)}) async-done(((bf16[1024,1536]{1,0:T(8,128)(2,1)}, bf16[512,1024]{1,0:T(8,128)(2,1)}, bf16[1024,4096]{1,0:T(8,128)(2,1)}, bf16[2048,1024]{1,0:T(8,128)(2,1)}), (bf16[1024,1536]{1,0:T(8,128)(2,1)}, bf16[512,1024]{1,0:T(8,128)(2,1)}, ...) | async-done | bytes 16777232 | tf_op jit(solution)/shard_map/psum | solution.py:253
  882.1 11.8 %fusion.92 = (f32[1024,2048]{1,0:T(8,128)}, f32[1024,2048]{1,0:T(8,128)}) fusion(bf16[1024,4096]{1,0:T(8,128)(2,1)} %get-tuple-element.610), kind=kLoop, calls=%fused_computation.175 | loop fusion | bytes 33554432 | tf_op jit(solution)/shard_map/slice | solution.py:273
  (252 shorter events, 170.3 us)
Async XLA Ops:
  7.2 107.4 %copy-start = (bf16[512,1024]{1,0:T(8,128)(2,1)S(1)}, bf16[512,1024]{1,0:T(8,128)(2,1)}, u32[]{:S(2)}) copy-start(bf16[512,1024]{1,0:T(8,128)(2,1)} %param.27) | copy-start | bytes 3145732
  7.2 4.0 copy-start.11
  7.2 4.0 copy-start.38
  7.2 4.0 copy-start.48
  7.2 18.8 %all-gather.5.cloned.1.call-start = ((), (), s32[]{:S(2)}) async-start(), calls=%async_computation.4 | async-start | bytes 3145728 | tf_op jit(solution)/shard_map/all_gather | solution.py:112
  8.9 3.8 copy-start.53
  8.9 4.0 copy-start.22
  12.6 119.8 %reduce-scatter.5.cloned.1.call-start = ((), (), s32[]{:S(2)}) async-start(), calls=%async_computation.5 | async-start | bytes 6291456 | tf_op jit(solution)/shard_map/reduce_scatter | solution.py:158
  12.8 43.7 %copy-start.42 = (f32[512]{0:T(512)}, f32[512]{0:T(512)S(1)}, u32[]{:S(2)}) copy-start(f32[512]{0:T(512)S(1)} %get-tuple-element.643) | copy-start | bytes 6148
  12.8 43.7 %copy-start.44 = (f32[512]{0:T(512)}, f32[512]{0:T(512)S(1)}, u32[]{:S(2)}) copy-start(f32[512]{0:T(512)S(1)} %get-tuple-element.644) | copy-start | bytes 6148
  15.9 40.6 %copy-start.33 = (f32[1024]{0:T(1024)}, f32[1024]{0:T(1024)S(1)}, u32[]{:S(2)}) copy-start(f32[1024]{0:T(1024)S(1)} %fusion.66) | copy-start | bytes 12292
  119.0 13.4 %copy-start.12 = (bf16[512,1024]{1,0:T(8,128)(2,1)S(1)}, bf16[512,1024]{1,0:T(8,128)(2,1)}, u32[]{:S(2)}) copy-start(bf16[512,1024]{1,0:T(8,128)(2,1)} %param.19) | copy-start | bytes 3145732
  119.0 30.0 %all-gather.7.cloned.1.call-start = ((), (), s32[]{:S(2)}) async-start(), calls=%async_computation.6 | async-start | bytes 3145728 | tf_op jit(solution)/shard_map/all_gather | solution.py:166
  137.0 28.5 %all-gather.9.cloned.1.call-start = ((), (), s32[]{:S(2)}) async-start(), calls=%async_computation.8 | async-start | bytes 3145728 | tf_op jit(solution)/shard_map/all_gather | solution.py:179
  137.6 72.7 %reduce-scatter.9.cloned.1.call-start = ((), (), s32[]{:S(2)}) async-start(), calls=%async_computation.9 | async-start | bytes 6291456 | tf_op jit(solution)/shard_map/reduce_scatter | solution.py:186
  137.7 5.0 copy-start.19
  196.9 27.1 %reduce-scatter.7.cloned.1.call-start = ((), (), s32[]{:S(2)}) async-start(), calls=%async_computation.7 | async-start | bytes 3145728 | tf_op jit(solution)/shard_map/reduce_scatter | solution.py:173
  206.2 17.8 %copy-start.18 = (bf16[512,1024]{1,0:T(8,128)(2,1)S(1)}, bf16[512,1024]{1,0:T(8,128)(2,1)}, u32[]{:S(2)}) copy-start(bf16[512,1024]{1,0:T(8,128)(2,1)} %param.33) | copy-start | bytes 3145732
  206.2 35.6 %all-gather.11.cloned.1.call-start = ((), (), s32[]{:S(2)}) async-start(), calls=%async_computation.10 | async-start | bytes 3145728 | tf_op jit(solution)/shard_map/all_gather | solution.py:194
  229.8 187.3 %reduce-scatter.11.cloned.1.call-start = ((), (), s32[]{:S(2)}) async-start(), calls=%async_computation.11 | async-start | bytes 3145728 | tf_op jit(solution)/shard_map/reduce_scatter | solution.py:241
  279.7 7.2 copy-start.2
  326.9 7.2 copy-start.2
  372.3 10.4 %copy-start.31 = (bf16[1024,1536]{1,0:T(8,128)(2,1)S(1)}, bf16[1024,1536]{1,0:T(8,128)(2,1)}, u32[]{:S(2)}) copy-start(bf16[1024,1536]{1,0:T(8,128)(2,1)} %copy-done.30) | copy-start | bytes 9437188
  387.4 482.9 %all-reduce.4.cloned.1.call-start = ((), (), s32[]{:S(2)}) async-start(), calls=%async_computation.12 | async-start | bytes 33554432 | tf_op jit(solution)/shard_map/psum | solution.py:253
  389.0 8.8 copy-start.51
  389.0 8.8 copy-start.55
  389.0 8.8 copy-start.56
  397.7 11.5 %copy-start.21 = (bf16[1024,1024]{1,0:T(8,128)(2,1)S(1)}, bf16[1024,1024]{1,0:T(8,128)(2,1)}, u32[]{:S(2)}) copy-start(bf16[1024,1024]{1,0:T(8,128)(2,1)} %all-gather.11.cloned.1.call-done) | copy-start | bytes 6291460
  397.7 11.5 %copy-start.25 = (bf16[2,512,512]{2,1,0:T(8,128)(2,1)S(1)}, bf16[2,512,512]{2,1,0:T(8,128)(2,1)}, u32[]{:S(2)}) copy-start(bf16[2,512,512]{2,1,0:T(8,128)(2,1)} %get-tuple-element.475) | copy-start | bytes 3145732
  418.3 46.7 %copy-start.20 = (bf16[512,1024]{1,0:T(8,128)(2,1)S(1)}, bf16[512,1024]{1,0:T(8,128)(2,1)}, u32[]{:S(2)}) copy-start(bf16[512,1024]{1,0:T(8,128)(2,1)} %reduce-scatter.11.cloned.1.call-done) | copy-start | bytes 3145732
  873.3 4.4 copy-start.17
  882.1 11.8 %copy-start.1 = (bf16[512,1024]{1,0:T(8,128)(2,1)S(1)}, bf16[512,1024]{1,0:T(8,128)(2,1)}, u32[]{:S(2)}) copy-start(bf16[512,1024]{1,0:T(8,128)(2,1)} %param.27) | copy-start | bytes 3145732
  (41 other events, 81.9 us)
Sparse Core Ops, SparseCore 0:
  12.7 13.2 all-gather.4
  119.2 13.2 reduce-scatter.4
  137.1 11.8 all-gather.6
  150.4 11.7 all-gather.8
  197.0 13.2 reduce-scatter.8
  212.9 11.0 reduce-scatter.6
  229.9 11.8 all-gather.10
  387.5 10.9 reduce-scatter.10
  417.2 453.0 all-reduce.3
where the time goes:
time: 906 us; the launch traced here: 901 us
  waiting for transfers between devices  456 us (50%)
  matrix products  167 us (18%)
  local copies, waits for them, and re-layouts  108 us (12%)
  other arithmetic  98.1 us (11%)
  blocking collectives  44.3 us (5%)
  between operations  14.8 us (2%)
  loops' own time  12.2 us (1%)
    psum x1, waiting for transfers between devices, on_device(): lax.psum(grad_qkv_w.astype(jnp.bfloat16), 'wide').astype(jnp.float32)  402 us
    psum x1, blocking collectives, on_device(): lax.psum((gain_one_grad, shift_one_grad, gain_two_grad, shift_two_grad),...  44.3 us
    dot_general x4, matrix products, times_transpose(): lax.dot_general(left, right, (((1,), (1,)), ((), ())), preferred_element_...  37.9 us
    dot_general x4, matrix products, transpose_times(): lax.dot_general(left, right, (((0,), (0,)), ((), ())), preferred_element_...  28 us
    convert_element_type x2, other arithmetic, attend_backward(): grad_scores = (attention_probs * (grad_probs - centre)).astype(jnp.bfloat16)  20.8 us
    dot_general x2, matrix products, attend_backward(): jnp.einsum('qhd,khd->hqk', grad_rows, value_pair, preferred_element_type=...  19.4 us
    unnamed x103, local copies, waits for them, and re-layouts  19.3 us
  transfers between devices with their start and end apart: 9, of which 7 were waited for; matrix products, arithmetic and copies ran while one was open for 8% of the time, Pallas kernels for 0%

commit v1 on v0

--- a/solution.py
+++ b/solution.py
@@ -7,6 +7,12 @@
 EPSILON = 1e-05
 MASKED = -1e30
 ROPE_BASE = 10000.0
+
+
+def link_wires(frame_in):
+    y = jax.lax.all_gather(frame_in, axis_name="wide")
+    known = jnp.sum(y, axis=0)
+    return known
 
 
 def times_transpose(left, right):
@@ -250,7 +256,7 @@
     )
     token_grad = grad_resid + grad_in_one
     qkv_summed, out_summed, gate_up_summed, down_summed = (
-        lax.psum(grad_qkv_w.astype(jnp.bfloat16), "wide").astype(jnp.float32),
+        link_wires(grad_qkv_w.astype(jnp.bfloat16)).astype(jnp.float32),
         lax.psum(grad_out_w.astype(jnp.bfloat16), "wide").astype(jnp.float32),
         lax.psum(grad_gate_up_w.astype(jnp.bfloat16), "wide").astype(jnp.float32),
         lax.psum(grad_down_w.astype(jnp.bfloat16), "wide").astype(jnp.float32),

time: 906 us -> 1350 us (1.49)
  waiting for transfers between devices: 456 us -> 866 us
  other arithmetic: 98.1 us -> 125 us
    all_gather x0 -> x1, waiting for transfers between devices: none -> 488 us  [link_wires(): y = jax.lax.all_gather(frame_in, axis_name='wide')]
    psum x1, waiting for transfers between devices: 402 us -> 325 us  [on_device(): lax.psum(grad_out_w.astype(jnp.bfloat16), 'wide').astype(jnp.float32)]
    reduce_sum x0 -> x1, other arithmetic: none -> 18.7 us  [link_wires(): known = jnp.sum(y, axis=0)]
  transfers between devices with their start and end apart: 9 -> 10, of which waited for: 7 -> 8; matrix products, arithmetic and copies ran while one was open for 8% -> 7% of each run, Pallas kernels for 0% -> 0%
where the time goes in v1:
time: 1350 us; the launch traced here: 1340 us
  waiting for transfers between devices  866 us (64%)
  matrix products  168 us (12%)
  other arithmetic  125 us (9%)
  local copies, waits for them, and re-layouts  109 us (8%)
  blocking collectives  44.2 us (3%)
  between operations  15.1 us (1%)
    all_gather x1, waiting for transfers between devices, link_wires(): y = jax.lax.all_gather(frame_in, axis_name='wide')  488 us
    psum x1, waiting for transfers between devices, on_device(): lax.psum(grad_out_w.astype(jnp.bfloat16), 'wide').astype(jnp.float32)  325 us
    psum x1, blocking collectives, on_device(): lax.psum((gain_one_grad, shift_one_grad, gain_two_grad, shift_two_grad),...  44.2 us
    dot_general x4, matrix products, times_transpose(): lax.dot_general(left, right, (((1,), (1,)), ((), ())), preferred_element_...  37.9 us
    dot_general x4, matrix products, transpose_times(): lax.dot_general(left, right, (((0,), (0,)), ((), ())), preferred_element_...  30.4 us
  transfers between devices with their start and end apart: 10, of which 8 were waited for; matrix products, arithmetic and copies ran while one was open for 7% of the time, Pallas kernels for 0%

profile of v1, /device:TPU:0, one launch (start us, length us, event | category | flops | bytes accessed | tf_op | source)
XLA Modules:
  0.0 1340.3 jit_solution(10902470049694580814)
XLA Ops:
  16.0 10.1 all-gather.7.cloned.1.call-done
  26.1 5.9 fusion.98
  51.2 10.9 fusion.54
  65.9 44.1 %while.36 = (s32[]{:T(128)}, bf16[2,512,512]{2,1,0:T(8,128)(2,1)}, f32[2,8,512]{2,1,0:T(8,128)}, s32[2]{0:T(128)S(1)}, s32[2]{0:T(128)S(1)}, /*index=5*/s32[2]{0...) while((s32[]{:T(128)}, bf16[2,512,512]{2,1,0:T(8,128)(2,1)}, ...), condition=%wide.region_5.6_spmd, body=%wide.region_2.5_spmd.sunk | while | flops 1111768064 | bytes 60953168 | solution.py:162
  114.8 13.1 reduce-scatter.5.cloned.1.call-done
  133.4 4.9 constant_dynamic-update-slice_fusion.6
  144.8 16.0 %fusion.100 = f32[1024,4096]{1,0:T(8,128)} fusion(bf16[1024,1024]{1,0:T(8,128)(2,1)} %all-gather.9.cloned.1.call-done, bf16[1024,4096]{1,0:T(8,128)(2,1)} %constant_dynamic-update-slice_fusion.5), kind=kOutput, calls=%fused_computation.183 | convolution fusion | flops 8589934592 | bytes 27262976 | tf_op jit(solution)/shard_map/dot_general | solution.py:174
  160.8 15.5 %multiply_convert_fusion.2 = (bf16[1024,2048]{1,0:T(8,128)(2,1)S(1)}, bf16[1024,2048]{1,0:T(8,128)(2,1)}, bf16[1024,2048]{1,0:T(8,128)(2,1)}) fusion(f32[1024,4096]{1,0:T(8,128)} %fusion.100, bf16[1024,1024]{1,0:T(8,128)(2,1)} %all-gather.11.cloned.1.call-done, bf16[2048,1024]{1,0:T(8,128)(2,1)} %param.32), kind=kOutput, calls=%fused_computation.59 | convolution fusion | flops 4328521728 | bytes 35651584 | tf_op jit(solution)/shard_map/dot_general | solution.py:19
  178.3 13.9 %fusion.31 = f32[1024,1024]{1,0:T(8,128)} fusion(bf16[1024,4096]{1,0:T(8,128)(2,1)} %constant_dynamic-update-slice_fusion.5, bf16[1024,2048]{1,0:T(8,128)(2,1)} %get-tuple-element.626, bf16[1024,2048]{1,0:T(8,128)(2,1)S(1)} %get-tuple-element.625), kind=kOutput, calls=%fused_computation.63 | convolution fusion | flops 8606711808 | bytes 20971520 | tf_op jit(solution)/shard_map/dot_general | solution.py:19
  192.7 9.3 convolution_convert_fusion.4
  209.3 10.1 reduce-scatter.7.cloned.1.call-done
  219.3 6.1 fusion.88
  225.5 11.9 all-gather.13.cloned.1.call-done
  242.9 102.3 %while.37 = (s32[]{:T(128)}, f32[1024,512]{1,0:T(8,128)}, f32[1024,512]{0,1:T(8,128)}, f32[1024,512]{0,1:T(8,128)}, s32[2]{0:T(128)S(1)}, /*index=5*/s32[2]{0:T(...) while((s32[]{:T(128)}, f32[1024,512]{1,0:T(8,128)}, ...), condition=%wide.region_15.16_spmd.clone, body=%wide.region_13.15_spmd.clone.sunk | while | flops 2736798720 | bytes 219271792 | solution.py:239
  255.7 9.7 multiply_reduce_fusion.6
  265.4 10.4 multiply_convert_fusion.5
  275.8 7.2 fusion.176
  306.1 9.7 multiply_reduce_fusion.6
  315.7 10.4 multiply_convert_fusion.5
  326.1 7.2 fusion.176
  349.2 9.4 fusion.61
  375.5 9.1 fusion.56
  390.7 9.5 convolution_convert_fusion.2
  400.2 11.7 convolution_convert_fusion
  415.7 6.9 convolution_convert_fusion.1
  426.1 44.2 %all-reduce = (f32[1024]{0:T(1024)}, f32[1024]{0:T(1024)}, f32[1024]{0:T(1024)}, f32[1024]{0:T(1024)}) all-reduce(f32[1024]{0:T(1024)S(1)} %get-tuple-element.559, f32[1024]{0:T(1024)S(1)} %get-tuple-element.563, f32[1024]{0:T(1024)S(1)} %copy-done.42, f32[1024]{0:T(1024)S(1)} %copy-done.43), channel_id=1, replica_groups=mesh['wide'=16,'narrow'=2] {'wide','narrow'}, use_global_device_ids=true, to_apply=%region_20.21 | all-reduce | flops 4096 | bytes 32768 | tf_op jit(solution)/shard_map/psum | solution.py:264
  473.6 325.2 %all-reduce.4.cloned.1.call-done = (bf16[512,1024]{1,0:T(8,128)(2,1)}, bf16[1024,4096]{1,0:T(8,128)(2,1)}, bf16[2048,1024]{1,0:T(8,128)(2,1)}) async-done(((bf16[512,1024]{1,0:T(8,128)(2,1)}, bf16[1024,4096]{1,0:T(8,128)(2,1)}, bf16[2048,1024]{1,0:T(8,128)(2,1)}), (bf16[512,1024]{1,0:T(8,128)(2,1)}, bf16[1024,4096]{1,0:T(8,128)(2,1)}, bf16[2048,1024]{1,0:T(8,128)(2,1)})) %all-reduce.4.cloned.1.call-update) | async-done | bytes 13631504 | tf_op jit(solution)/shard_map/psum | solution.py:260
  801.6 6.6 convert_element_type.154
  808.3 13.4 fusion.92
  821.6 487.6 %all-gather.15.cloned.1.call-done = bf16[16384,1536]{1,0:T(8,128)(2,1)} async-done(((bf16[1024,1536]{1,0:T(8,128)(2,1)}), bf16[16384,1536]{1,0:T(8,128)(2,1)}) %all-gather.15.cloned.1.call-update) | async-done | bytes 50331664 | tf_op jit(solution)/shard_map/all_gather | solution.py:13
  1309.3 18.7 %reduce_sum.160 = bf16[1024,1536]{1,0:T(8,128)(2,1)} reduce(bf16[16,1024,1536]{2,1,0:T(8,128)(2,1)} %bitcast.145, bf16[]{:T(256)} %constant.365.clone.1), dimensions={0}, to_apply=%region_23.24 | reduce | flops 23592960 | bytes 53477376 | tf_op jit(solution)/shard_map/reduce_sum | solution.py:14
  1328.0 5.0 fusion.94
  (242 shorter events, 183.5 us)
Async XLA Ops:
  7.2 102.8 %copy-start = (bf16[512,1024]{1,0:T(8,128)(2,1)S(1)}, bf16[512,1024]{1,0:T(8,128)(2,1)}, u32[]{:S(2)}) copy-start(bf16[512,1024]{1,0:T(8,128)(2,1)} %param.27) | copy-start | bytes 3145732
  7.2 4.0 copy-start.10
  7.2 4.0 copy-start.34
  7.2 4.0 copy-start.44
  7.2 18.9 %all-gather.7.cloned.1.call-start = ((), (), s32[]{:S(2)}) async-start(), calls=%async_computation.4 | async-start | bytes 3145728 | tf_op jit(solution)/shard_map/all_gather | solution.py:118
  8.9 3.9 copy-start.47
  8.9 4.0 copy-start.18
  12.7 115.2 %reduce-scatter.5.cloned.1.call-start = ((), (), s32[]{:S(2)}) async-start(), calls=%async_computation.5 | async-start | bytes 6291456 | tf_op jit(solution)/shard_map/reduce_scatter | solution.py:164
  12.9 38.3 %copy-start.38 = (f32[512]{0:T(512)}, f32[512]{0:T(512)S(1)}, u32[]{:S(2)}) copy-start(f32[512]{0:T(512)S(1)} %get-tuple-element.642) | copy-start | bytes 6148
  12.9 38.3 %copy-start.40 = (f32[512]{0:T(512)}, f32[512]{0:T(512)S(1)}, u32[]{:S(2)}) copy-start(f32[512]{0:T(512)S(1)} %get-tuple-element.643) | copy-start | bytes 6148
  16.0 35.2 %copy-start.29 = (f32[1024]{0:T(1024)}, f32[1024]{0:T(1024)S(1)}, u32[]{:S(2)}) copy-start(f32[1024]{0:T(1024)S(1)} %fusion.66) | copy-start | bytes 12292
  114.5 30.3 %all-gather.9.cloned.1.call-start = ((), (), s32[]{:S(2)}) async-start(), calls=%async_computation.6 | async-start | bytes 3145728 | tf_op jit(solution)/shard_map/all_gather | solution.py:172
  132.8 28.0 %all-gather.11.cloned.1.call-start = ((), (), s32[]{:S(2)}) async-start(), calls=%async_computation.8 | async-start | bytes 3145728 | tf_op jit(solution)/shard_map/all_gather | solution.py:185
  133.3 72.2 %reduce-scatter.9.cloned.1.call-start = ((), (), s32[]{:S(2)}) async-start(), calls=%async_computation.9 | async-start | bytes 6291456 | tf_op jit(solution)/shard_map/reduce_scatter | solution.py:192
  133.4 5.0 copy-start.16
  192.2 27.1 %reduce-scatter.7.cloned.1.call-start = ((), (), s32[]{:S(2)}) async-start(), calls=%async_computation.7 | async-start | bytes 3145728 | tf_op jit(solution)/shard_map/reduce_scatter | solution.py:179
  202.0 35.5 %all-gather.13.cloned.1.call-start = ((), (), s32[]{:S(2)}) async-start(), calls=%async_computation.10 | async-start | bytes 3145728 | tf_op jit(solution)/shard_map/all_gather | solution.py:200
  225.5 197.2 %reduce-scatter.11.cloned.1.call-start = ((), (), s32[]{:S(2)}) async-start(), calls=%async_computation.11 | async-start | bytes 3145728 | tf_op jit(solution)/shard_map/reduce_scatter | solution.py:247
  275.8 7.2 copy-start.2
  285.2 4.5 copy-start.4
  326.1 7.2 copy-start.2
  335.5 5.9 copy-start.4
  375.5 10.4 copy-start.27
  390.6 9.6 copy-start.46
  390.6 408.3 %all-reduce.4.cloned.1.call-start = ((), (), s32[]{:S(2)}) async-start(), calls=%async_computation.13 | async-start | bytes 27262976 | tf_op jit(solution)/shard_map/psum | solution.py:260
  390.6 9.6 copy-start.49
  390.6 9.6 copy-start.50
  400.2 11.7 copy-start.17
  400.2 11.7 copy-start.21
  414.2 895.1 %all-gather.15.cloned.1.call-start = ((), (), s32[]{:S(2)}) async-start(), calls=%async_computation.12 | async-start | bytes 53477376 | tf_op jit(solution)/shard_map/all_gather | solution.py:13
  422.7 47.7 %copy-start.14 = (f32[512,1024]{1,0:T(8,128)S(1)}, f32[512,1024]{1,0:T(8,128)}, u32[]{:S(2)}) copy-start(f32[512,1024]{1,0:T(8,128)} %get-tuple-element.612) | copy-start | bytes 6291460
  1328.0 5.0 copy-start.1
  (35 other events, 67.0 us)
Sparse Core Ops, SparseCore 0:
  12.8 13.2 all-gather.6
  114.7 13.2 reduce-scatter.4
  132.9 11.8 all-gather.8
  146.2 11.7 all-gather.10
  192.3 13.2 reduce-scatter.8
  208.3 11.0 reduce-scatter.6
  225.6 11.8 all-gather.12
  390.7 10.9 reduce-scatter.10
  414.3 384.4 all-reduce.3
  801.5 507.7 all-gather.14
